TPU v7x, 32 devices: a whole 2x2x4 slice. The times are simulated.
32 devices in a mesh: row: 8 (over y, x, core), col: 4 (over z).
Axes of the slice: x: 2, y: 2, z: 4, core: 2. Of those that a mesh axis runs over, the one named last changes fastest.
Arguments:
- student_in: bfloat16 [768, 8192], P('col', 'row'), may hold values from -6 to 6
- norm_gain: bfloat16 [8192], P('row'), may hold values from 0.099609375 to 1.8984375
- w_gate: bfloat16 [8192, 28672], P('row', 'col'), may hold values from -0.0625 to 0.0625
- w_up: bfloat16 [8192, 28672], P('row', 'col'), may hold values from -0.0625 to 0.0625
- w_down: bfloat16 [28672, 8192], P('col', 'row'), may hold values from -0.03125 to 0.03125
- teacher: bfloat16 [2, 768, 8192], P(None, 'col', 'row'), may hold values from -6 to 6
- layer_map: int32 [2], replicated, may hold values from 0 to 1, each once
Outputs:
- student_out: bfloat16 [768, 8192], P('col', 'row')
- match_loss: float32 [], replicated
Inputs may be any that keep to these rules, and one draw needn't show every extreme that they name: `layer_map`: a permutation of 0 to 1.
All inputs are finite; a program needn't handle non-finite values.
Results may differ from a plain program's by a relative error of at most 0.014.
Values may be sent and summed in bfloat16 or wider, within the bound.
A program may use at most 192 MiB of HBM per device.

v0:
```python
import jax
import jax.numpy as jnp
from jax import lax
from jax.sharding import PartitionSpec as P

D = 8192


def swiglu(both, width):
    return (jax.nn.silu(both[:, :width]) * both[:, width:]).astype(jnp.bfloat16)


def body(student_in, norm_gain, w_gate, w_up, w_down, teacher, layer_map):
    xf = student_in.astype(jnp.float32)
    squares = lax.psum(jnp.sum(xf * xf, axis=1), "row")
    mean_sq = squares / D
    normed = (
        xf * lax.rsqrt(mean_sq[:, None] + 1e-05) * norm_gain.astype(jnp.float32)[None, :]
    ).astype(jnp.bfloat16)
    all_rows = lax.all_gather(normed, "col", axis=0, tiled=True)
    width = w_gate.shape[1]
    piece = all_rows
    first = jnp.dot(piece, w_gate, preferred_element_type=jnp.float32)
    second = jnp.dot(piece, w_up, preferred_element_type=jnp.float32)
    mine = lax.psum_scatter(
        jnp.concatenate([first, second], axis=1).astype(jnp.bfloat16),
        "row",
        scatter_dimension=0,
        tiled=True,
    ).astype(jnp.float32)
    hidden_all = lax.all_gather(swiglu(mine, width), "row", axis=0, tiled=True)
    piece = hidden_all
    branch = lax.psum_scatter(
        jnp.dot(piece, w_down, preferred_element_type=jnp.float32).astype(jnp.bfloat16),
        "col",
        scatter_dimension=0,
        tiled=True,
    ).astype(jnp.float32)
    student_out = (xf + branch).astype(jnp.bfloat16)
    target = lax.dynamic_index_in_dim(teacher, layer_map[0], 0, keepdims=False).astype(jnp.float32)
    diff = student_out.astype(jnp.float32) - target
    total = lax.psum(jnp.sum(diff * diff), ("row", "col"))
    count_all = student_in.shape[0] * lax.axis_size("col") * D
    return (student_out, total / count_all)


def solution(mesh):
    placed = (
        P("col", "row"),
        P("row"),
        P("row", "col"),
        P("row", "col"),
        P("col", "row"),
        P(None, "col", "row"),
        P(),
    )
    return jax.shard_map(
        body, mesh=mesh, in_specs=placed, out_specs=(P("col", "row"), P()), check_vma=False
    )
```

profile of v0, /device:TPU:0, one launch (start us, length us, event | category | flops | bytes accessed | tf_op | source)
XLA Modules:
  0.0 428.6 jit_solution(13553694904345614874)
XLA Ops:
  7.2 0.0 all-gather.3.cloned.1.call-start
  7.2 1.2 fusion.1
  8.4 15.1 %psum.14 = f32[192]{0:T(256)S(1)} all-reduce(f32[192]{0:T(256)S(1)} %fusion.1), channel_id=1, replica_groups=mesh['row'=8,'col'=4] {'row'}, use_global_device_ids=true, to_apply=%region_1.0 | all-reduce | flops 192 | bytes 1536 | tf_op jit(solution)/shard_map/psum | solution.py:15
  23.5 0.7 convert_element_type.35
  24.2 1.9 fusion.3
  26.1 0.0 all-gather.3.cloned.1.call-update
  26.1 0.0 reduce-scatter.3.cloned.1.call-start
  26.2 36.5 %all-gather.3.cloned.1.call-done = bf16[768,1024]{1,0:T(8,128)(2,1)} async-done(((bf16[192,1024]{1,0:T(8,128)(2,1)}), bf16[768,1024]{1,0:T(8,128)(2,1)}) %all-gather.3.cloned.1.call-update) | async-done | bytes 1572880 | tf_op jit(solution)/shard_map/all_gather | solution.py:20
  62.7 0.0 copy-start.3
  62.7 17.3 %convolution_convert_fusion = bf16[768,7168]{1,0:T(8,128)(2,1)S(1)} fusion(bf16[768,1024]{1,0:T(8,128)(2,1)} %all-gather.3.cloned.1.call-done, bf16[1024,7168]{1,0:T(8,128)(2,1)} %param.10), kind=kOutput, calls=%fused_computation.1 | convolution fusion | flops 11279794176 | bytes 27262976 | tf_op jit(solution)/shard_map/dot_general | solution.py:24
  79.9 0.0 copy-done.3
  80.0 19.0 %convolution_convert_fusion.1 = bf16[768,7168]{1,0:T(8,128)(2,1)} fusion(bf16[768,1024]{1,0:T(8,128)(2,1)S(1)} %copy-done.3, bf16[1024,7168]{1,0:T(8,128)(2,1)} %param.9), kind=kOutput, calls=%fused_computation.2 | convolution fusion | flops 11279794176 | bytes 27262976 | tf_op jit(solution)/shard_map/dot_general | solution.py:23
  98.9 16.5 %pad_maximum_fusion = bf16[768,14336]{1,0:T(8,128)(2,1)} fusion(bf16[768,7168]{1,0:T(8,128)(2,1)S(1)} %convolution_convert_fusion, bf16[768,7168]{1,0:T(8,128)(2,1)} %convolution_convert_fusion.1), kind=kLoop, calls=%fused_computation | loop fusion | flops 44040192 | bytes 44040192 | tf_op jit(solution)/shard_map/concatenate | solution.py:26
  115.4 0.0 reduce-scatter.3.cloned.1.call-update
  115.4 0.0 all-gather.5.cloned.1.call-start
  115.5 140.1 %reduce-scatter.3.cloned.1.call-done = bf16[96,14336]{1,0:T(8,128)(2,1)} async-done(((bf16[768,14336]{1,0:T(8,128)(2,1)}), bf16[96,14336]{1,0:T(8,128)(2,1)}) %reduce-scatter.3.cloned.1.call-update) | async-done | bytes 2752528 | tf_op jit(solution)/shard_map/reduce_scatter | solution.py:25
  255.5 2.3 convert_element_type.37
  257.8 1.8 fusion
  259.6 0.0 all-gather.5.cloned.1.call-update
  259.6 0.0 copy-start.2
  259.6 0.0 copy-start
  259.6 0.0 copy-start.1
  259.6 0.2 reduce-scatter.5.cloned.1.call-start
  259.9 65.2 %all-gather.5.cloned.1.call-done = bf16[768,7168]{1,0:T(8,128)(2,1)} async-done(((bf16[96,7168]{1,0:T(8,128)(2,1)}), bf16[768,7168]{1,0:T(8,128)(2,1)}) %all-gather.5.cloned.1.call-update) | async-done | bytes 11010064 | tf_op jit(solution)/shard_map/all_gather | solution.py:31
  325.1 17.8 %convolution_convert_fusion.2 = bf16[768,1024]{1,0:T(8,128)(2,1)} fusion(bf16[768,7168]{1,0:T(8,128)(2,1)} %all-gather.5.cloned.1.call-done, bf16[7168,1024]{1,0:T(8,128)(2,1)} %param.11), kind=kOutput, calls=%fused_computation.5 | convolution fusion | flops 11275075584 | bytes 27262976 | tf_op jit(solution)/shard_map/dot_general | solution.py:34
  342.9 0.0 reduce-scatter.5.cloned.1.call-update
  342.9 0.0 copy-done.2
  343.0 35.5 %reduce-scatter.5.cloned.1.call-done = bf16[192,1024]{1,0:T(8,128)(2,1)} async-done(((bf16[768,1024]{1,0:T(8,128)(2,1)}), bf16[192,1024]{1,0:T(8,128)(2,1)}) %reduce-scatter.5.cloned.1.call-update) | async-done | bytes 393232 | tf_op jit(solution)/shard_map/reduce_scatter | solution.py:33
  378.5 0.0 copy-done
  378.5 0.0 copy-done.1
  378.5 2.5 fusion.6
  381.0 39.2 %psum.15 = f32[]{:T(128)} all-reduce(f32[]{:T(128)} %get-tuple-element.2), channel_id=1, replica_groups=mesh['row'=8,'col'=4] {'row','col'}, use_global_device_ids=true, to_apply=%region_5.6 | all-reduce | flops 1 | bytes 8 | tf_op jit(solution)/shard_map/psum | solution.py:42
  (1 shorter events, 0.0 us)
Async XLA Ops:
  7.2 55.5 %all-gather.3.cloned.1.call-start = ((), (), s32[]{:S(2)}) async-start(), calls=%async_computation.2 | async-start | bytes 1966080 | tf_op jit(solution)/shard_map/all_gather | solution.py:20
  26.1 229.4 %reduce-scatter.3.cloned.1.call-start = ((), (), s32[]{:S(2)}) async-start(), calls=%async_computation.3 | async-start | bytes 24772608 | tf_op jit(solution)/shard_map/reduce_scatter | solution.py:25
  62.7 17.3 %copy-start.3 = (bf16[768,1024]{1,0:T(8,128)(2,1)S(1)}, bf16[768,1024]{1,0:T(8,128)(2,1)}, u32[]{:S(2)}) copy-start(bf16[768,1024]{1,0:T(8,128)(2,1)} %all-gather.3.cloned.1.call-done) | copy-start | bytes 4718596
  115.4 209.7 %all-gather.5.cloned.1.call-start = ((), (), s32[]{:S(2)}) async-start(), calls=%async_computation.4 | async-start | bytes 12386304 | tf_op jit(solution)/shard_map/all_gather | solution.py:31
  259.6 83.3 %copy-start.2 = (s32[2]{0:T(128)S(1)}, s32[2]{0:T(128)}, u32[]{:S(2)}) copy-start(s32[2]{0:T(128)} %param.13) | copy-start | bytes 28
  259.6 118.9 %copy-start = (bf16[192,1024]{1,0:T(8,128)(2,1)S(1)}, bf16[192,1024]{1,0:T(8,128)(2,1)}, u32[]{:S(2)}) copy-start(bf16[192,1024]{1,0:T(8,128)(2,1)} %param.7) | copy-start | bytes 1179652
  259.6 118.9 %copy-start.1 = (bf16[2,192,1024]{2,1,0:T(8,128)(2,1)S(1)}, bf16[2,192,1024]{2,1,0:T(8,128)(2,1)}, u32[]{:S(2)}) copy-start(bf16[2,192,1024]{2,1,0:T(8,128)(2,1)} %param.12) | copy-start | bytes 2359300
  259.6 118.8 %reduce-scatter.5.cloned.1.call-start = ((), (), s32[]{:S(2)}) async-start(), calls=%async_computation.5 | async-start | bytes 1966080 | tf_op jit(solution)/shard_map/reduce_scatter | solution.py:33
Sparse Core Ops, SparseCore 0:
  26.3 36.3 all-gather.2
  115.5 139.9 reduce-scatter.2
  259.7 65.3 all-gather.4
  343.0 35.4 reduce-scatter.4
where the time goes:
time: 429 us
  waiting for transfers between devices  277 us (65%)
  blocking collectives  54.4 us (13%)
  matrix products  54 us (13%)
  other arithmetic  26.8 us (6%)
  between operations  15.7 us (4%)
    reduce_scatter x1, waiting for transfers between devices, body(): lax.psum_scatter(jnp.concatenate([first, second], axis=1).astype(jnp.bflo...  140 us
    all_gather x1, waiting for transfers between devices, body(): hidden_all = lax.all_gather(swiglu(mine, width), 'row', axis=0, tiled=True)  65.2 us
    psum x1, blocking collectives, body(): total = lax.psum(jnp.sum(diff * diff), ('row', 'col'))  39.2 us
    all_gather x1, waiting for transfers between devices, body(): all_rows = lax.all_gather(normed, 'col', axis=0, tiled=True)  36.5 us
    reduce_scatter x1, waiting for transfers between devices, body(): lax.psum_scatter(jnp.dot(piece, w_down, preferred_element_type=jnp.float3...  35.5 us
    dot_general x1, matrix products, body(): first = jnp.dot(piece, w_gate, preferred_element_type=jnp.float32)  19 us
    dot_general x1, matrix products, body(): jnp.dot(piece, w_down, preferred_element_type=jnp.float32)  17.8 us
    dot_general x1, matrix products, body(): second = jnp.dot(piece, w_up, preferred_element_type=jnp.float32)  17.3 us
  transfers between devices with their start and end apart: 4, of which 4 were waited for; matrix products, arithmetic and copies ran while one was open for 0% of the time, Pallas kernels for 0%

commit v1 on v0

--- a/solution.py
+++ b/solution.py
@@ -17,7 +17,22 @@
     normed = (
         xf * lax.rsqrt(mean_sq[:, None] + 1e-05) * norm_gain.astype(jnp.float32)[None, :]
     ).astype(jnp.bfloat16)
-    all_rows = lax.all_gather(normed, "col", axis=0, tiled=True)
+
+    def windows_end(join_dim, here_x):
+        dev_axis = "col"
+        n_slots = lax.psum(1, dev_axis)
+        o_now = [(src_i - 1, src_i) for src_i in range(1, n_slots)] + [(n_slots - 1, 0)]
+        newest = here_x
+        grid = [newest]
+        for _ in tuple(range(n_slots - 1)):
+            newest = lax.ppermute(newest, dev_axis, o_now)
+            grid += [newest]
+        new = jnp.concatenate([*reversed(grid)], axis=join_dim)
+        return jnp.roll(
+            new, shift=(lax.axis_index(dev_axis) + 1) * newest.shape[join_dim], axis=join_dim
+        )
+
+    all_rows = windows_end(0, normed)
     width = w_gate.shape[1]
     piece = all_rows
     first = jnp.dot(piece, w_gate, preferred_element_type=jnp.float32)

time: 429 us -> 429 us (level)
  local copies, waits for them, and re-layouts: 0.02 us -> 4.66 us
    all_gather x1 -> x0, waiting for transfers between devices: 36.5 us -> none  [body(): all_rows = lax.all_gather(normed, 'col', axis=0, tiled=True)]
    ppermute x0 -> x3, waiting for transfers between devices: none -> 28.9 us  [windows_end(): newest = lax.ppermute(newest, dev_axis, o_now)]
    unnamed x8 -> x12, local copies, waits for them, and re-layouts: 0.02 us -> 4.66 us
  transfers between devices with their start and end apart: 4 -> 6, of which waited for: 4 -> 6; matrix products, arithmetic and copies ran while one was open for 0% -> 0% of each run, Pallas kernels for 0% -> 0%
where the time goes in v1:
time: 429 us
  waiting for transfers between devices  274 us (64%)
  blocking collectives  54.4 us (13%)
  matrix products  50.7 us (12%)
  other arithmetic  27.7 us (6%)
  between operations  15.7 us (4%)
  local copies, waits for them, and re-layouts  4.66 us (1%)
    reduce_scatter x1, waiting for transfers between devices, body(): lax.psum_scatter(jnp.concatenate([first, second], axis=1).astype(jnp.bflo...  144 us
    all_gather x1, waiting for transfers between devices, body(): hidden_all = lax.all_gather(swiglu(mine, width), 'row', axis=0, tiled=True)  65.3 us
    psum x1, blocking collectives, body(): total = lax.psum(jnp.sum(diff * diff), ('row', 'col'))  39.2 us
    reduce_scatter x1, waiting for transfers between devices, body(): lax.psum_scatter(jnp.dot(piece, w_down, preferred_element_type=jnp.float3...  35.5 us
    ppermute x3, waiting for transfers between devices, windows_end(): newest = lax.ppermute(newest, dev_axis, o_now)  28.9 us
    dot_general x1, matrix products, body(): jnp.dot(piece, w_down, preferred_element_type=jnp.float32)  17.8 us
    dot_general x1, matrix products, body(): second = jnp.dot(piece, w_up, preferred_element_type=jnp.float32)  17.7 us
    concatenate x1, other arithmetic, body(): jnp.concatenate([first, second], axis=1).astype(jnp.bfloat16)  16.2 us
  transfers between devices with their start and end apart: 6, of which 6 were waited for; matrix products, arithmetic and copies ran while one was open for 0% of the time, Pallas kernels for 0%

profile of v1, /device:TPU:0, one launch (start us, length us, event | category | flops | bytes accessed | tf_op | source)
XLA Modules:
  0.0 428.7 jit_solution(9844173093033122962)
XLA Ops:
  7.2 0.0 copy-start
  7.2 0.0 reduce-scatter.3.cloned.1.call-start
  7.2 0.7 convert_element_type.35
  7.9 1.2 fusion.3
  9.1 15.1 %psum.14 = f32[192]{0:T(256)S(1)} all-reduce(f32[192]{0:T(256)S(1)} %fusion.3), channel_id=1, replica_groups=mesh['row'=8,'col'=4] {'row'}, use_global_device_ids=true, to_apply=%region_1.0 | all-reduce | flops 192 | bytes 1536 | tf_op jit(solution)/shard_map/psum | solution.py:15
  24.3 1.2 fusion.5
  25.4 1.6 collective-permute-start
  27.0 9.3 %collective-permute-done = bf16[192,1024]{1,0:T(8,128)(2,1)S(1)} collective-permute-done((bf16[192,1024]{1,0:T(8,128)(2,1)S(1)}, bf16[192,1024]{1,0:T(8,128)(2,1)S(1)}, u32[]{:S(2)}, u32[]{:S(2)}) %collective-permute-start) | collective-permute-done | bytes 393248 | tf_op jit(solution)/shard_map/ppermute | solution.py:28
  36.3 0.0 collective-permute-start.1
  36.3 10.0 %collective-permute-done.1 = bf16[192,1024]{1,0:T(8,128)(2,1)S(1)} collective-permute-done((bf16[192,1024]{1,0:T(8,128)(2,1)S(1)}, bf16[192,1024]{1,0:T(8,128)(2,1)S(1)}, u32[]{:S(2)}, u32[]{:S(2)}) %collective-permute-start.1) | collective-permute-done | bytes 393248 | tf_op jit(solution)/shard_map/ppermute | solution.py:28
  46.3 0.0 collective-permute-start.2
  46.4 9.6 %collective-permute-done.2 = bf16[192,1024]{1,0:T(8,128)(2,1)S(1)} collective-permute-done((bf16[192,1024]{1,0:T(8,128)(2,1)S(1)}, bf16[192,1024]{1,0:T(8,128)(2,1)S(1)}, u32[]{:S(2)}, u32[]{:S(2)}) %collective-permute-start.2) | collective-permute-done | bytes 393248 | tf_op jit(solution)/shard_map/ppermute | solution.py:28
  55.9 0.8 constant_dynamic-update-slice_fusion.7
  56.7 0.8 constant_dynamic-update-slice_fusion.6
  57.5 0.8 constant_dynamic-update-slice_fusion.5
  58.2 0.0 copy-done
  58.2 0.9 constant_dynamic-update-slice_fusion.4
  59.2 0.8 constant_dynamic-update-slice_fusion.3
  59.9 0.8 constant_dynamic-update-slice_fusion.2
  60.7 0.8 constant_dynamic-update-slice_fusion.1
  61.5 0.9 constant_dynamic-update-slice_fusion
  62.4 15.2 %convolution_convert_fusion.1 = bf16[768,7168]{1,0:T(8,128)(2,1)S(1)} fusion(bf16[1024,7168]{1,0:T(8,128)(2,1)} %param.9, bf16[1536,1024]{1,0:T(8,128)(2,1)} %constant_dynamic-update-slice_fusion, s32[]{:T(128)S(6)} %select_n.18), kind=kOutput, calls=%fused_computation.2 | convolution fusion | flops 11279794176 | bytes 27262980 | tf_op jit(solution)/shard_map/dot_general | solution.py:38
  77.7 17.7 %convolution_convert_fusion = bf16[768,7168]{1,0:T(8,128)(2,1)} fusion(bf16[1024,7168]{1,0:T(8,128)(2,1)} %param.10, bf16[1536,1024]{1,0:T(8,128)(2,1)} %constant_dynamic-update-slice_fusion, s32[]{:T(128)S(6)} %select_n.18), kind=kOutput, calls=%fused_computation.1 | convolution fusion | flops 11279794176 | bytes 27262980 | tf_op jit(solution)/shard_map/dot_general | solution.py:39
  95.3 16.2 %pad_maximum_fusion = bf16[768,14336]{1,0:T(8,128)(2,1)} fusion(bf16[768,7168]{1,0:T(8,128)(2,1)} %convolution_convert_fusion, bf16[768,7168]{1,0:T(8,128)(2,1)S(1)} %convolution_convert_fusion.1), kind=kLoop, calls=%fused_computation | loop fusion | flops 44040192 | bytes 44040192 | tf_op jit(solution)/shard_map/concatenate | solution.py:41
  111.5 0.0 reduce-scatter.3.cloned.1.call-update
  111.6 0.0 all-gather.2.cloned.1.call-start
  111.6 144.1 %reduce-scatter.3.cloned.1.call-done = bf16[96,14336]{1,0:T(8,128)(2,1)} async-done(((bf16[768,14336]{1,0:T(8,128)(2,1)}), bf16[96,14336]{1,0:T(8,128)(2,1)}) %reduce-scatter.3.cloned.1.call-update) | async-done | bytes 2752528 | tf_op jit(solution)/shard_map/reduce_scatter | solution.py:40
  255.7 2.3 convert_element_type.37
  258.0 1.8 fusion
  259.8 0.0 all-gather.2.cloned.1.call-update
  259.8 0.0 copy-start.2
  259.8 0.0 copy-start.1
  259.8 0.2 reduce-scatter.5.cloned.1.call-start
  260.0 65.3 %all-gather.2.cloned.1.call-done = bf16[768,7168]{1,0:T(8,128)(2,1)} async-done(((bf16[96,7168]{1,0:T(8,128)(2,1)}), bf16[768,7168]{1,0:T(8,128)(2,1)}) %all-gather.2.cloned.1.call-update) | async-done | bytes 11010064 | tf_op jit(solution)/shard_map/all_gather | solution.py:46
  325.3 17.8 %convolution_convert_fusion.2 = bf16[768,1024]{1,0:T(8,128)(2,1)} fusion(bf16[768,7168]{1,0:T(8,128)(2,1)} %all-gather.2.cloned.1.call-done, bf16[7168,1024]{1,0:T(8,128)(2,1)} %param.11), kind=kOutput, calls=%fused_computation.5 | convolution fusion | flops 11275075584 | bytes 27262976 | tf_op jit(solution)/shard_map/dot_general | solution.py:49
  343.1 0.0 reduce-scatter.5.cloned.1.call-update
  343.1 0.0 copy-done.2
  343.2 35.5 %reduce-scatter.5.cloned.1.call-done = bf16[192,1024]{1,0:T(8,128)(2,1)} async-done(((bf16[768,1024]{1,0:T(8,128)(2,1)}), bf16[192,1024]{1,0:T(8,128)(2,1)}) %reduce-scatter.5.cloned.1.call-update) | async-done | bytes 393232 | tf_op jit(solution)/shard_map/reduce_scatter | solution.py:48
  378.7 0.0 copy-done.1
  378.7 2.5 fusion.8
  381.2 39.2 %psum.15 = f32[]{:T(128)} all-reduce(f32[]{:T(128)} %get-tuple-element.2), channel_id=1, replica_groups=mesh['row'=8,'col'=4] {'row','col'}, use_global_device_ids=true, to_apply=%region_5.6 | all-reduce | flops 1 | bytes 8 | tf_op jit(solution)/shard_map/psum | solution.py:57
  (1 shorter events, 0.0 us)
Async XLA Ops:
  7.2 51.1 %copy-start = (bf16[192,1024]{1,0:T(8,128)(2,1)S(1)}, bf16[192,1024]{1,0:T(8,128)(2,1)}, u32[]{:S(2)}) copy-start(bf16[192,1024]{1,0:T(8,128)(2,1)} %param.7) | copy-start | bytes 1179652
  7.2 248.5 %reduce-scatter.3.cloned.1.call-start = ((), (), s32[]{:S(2)}) async-start(), calls=%async_computation.2 | async-start | bytes 24772608 | tf_op jit(solution)/shard_map/reduce_scatter | solution.py:40
  25.4 10.9 %collective-permute-start = (bf16[192,1024]{1,0:T(8,128)(2,1)S(1)}, bf16[192,1024]{1,0:T(8,128)(2,1)S(1)}, u32[]{:S(2)}, u32[]{:S(2)}) collective-permute-start(bf16[192,1024]{1,0:T(8,128)(2,1)S(1)} %fusion.5), channel_id=1, source_target_pairs={{0,1},{1,2},{2,3},{3,0},{4,5},{5,6},{6,7},{7,4},{8,9},{9,10},{10,1... | collective-permute-start | bytes 1179656 | tf_op jit(solution)/shard_map/ppermute | solution.py:28
  36.3 10.0 %collective-permute-start.1 = (bf16[192,1024]{1,0:T(8,128)(2,1)S(1)}, bf16[192,1024]{1,0:T(8,128)(2,1)S(1)}, u32[]{:S(2)}, u32[]{:S(2)}) collective-permute-start(bf16[192,1024]{1,0:T(8,128)(2,1)S(1)} %collective-permute-done), channel_id=1, source_target_pairs={{0,1},{1,2},{2,3},{3,0},{4,5},{5,6},{6,7},{7,4},{8,9},{9,10},{10,1... | collective-permute-start | bytes 1179656 | tf_op jit(solution)/shard_map/ppermute | solution.py:28
  46.3 9.6 %collective-permute-start.2 = (bf16[192,1024]{1,0:T(8,128)(2,1)S(1)}, bf16[192,1024]{1,0:T(8,128)(2,1)S(1)}, u32[]{:S(2)}, u32[]{:S(2)}) collective-permute-start(bf16[192,1024]{1,0:T(8,128)(2,1)S(1)} %collective-permute-done.1), channel_id=1, source_target_pairs={{0,1},{1,2},{2,3},{3,0},{4,5},{5,6},{6,7},{7,4},{8,9},{9,10},{10,1... | collective-permute-start | bytes 1179656 | tf_op jit(solution)/shard_map/ppermute | solution.py:28
  111.6 213.7 %all-gather.2.cloned.1.call-start = ((), (), s32[]{:S(2)}) async-start(), calls=%async_computation.3 | async-start | bytes 12386304 | tf_op jit(solution)/shard_map/all_gather | solution.py:46
  259.8 83.3 %copy-start.2 = (s32[2]{0:T(128)S(1)}, s32[2]{0:T(128)}, u32[]{:S(2)}) copy-start(s32[2]{0:T(128)} %param.13) | copy-start | bytes 28
  259.8 118.9 %copy-start.1 = (bf16[2,192,1024]{2,1,0:T(8,128)(2,1)S(1)}, bf16[2,192,1024]{2,1,0:T(8,128)(2,1)}, u32[]{:S(2)}) copy-start(bf16[2,192,1024]{2,1,0:T(8,128)(2,1)} %param.12) | copy-start | bytes 2359300
  259.8 118.9 %reduce-scatter.5.cloned.1.call-start = ((), (), s32[]{:S(2)}) async-start(), calls=%async_computation.4 | async-start | bytes 1966080 | tf_op jit(solution)/shard_map/reduce_scatter | solution.py:48
Sparse Core Ops, SparseCore 0:
  111.7 143.9 reduce-scatter.2
  259.9 65.3 all-gather.1
  343.2 35.4 reduce-scatter.4
